TPU v7x, 32 devices: a whole 2x2x4 slice. The times are simulated.
32 devices in a mesh: dp: 8 (over z, x), tensor: 4 (over y, core).
Axes of the slice: x: 2, y: 2, z: 4, core: 2. Of those that a mesh axis runs over, the one named last changes fastest.
Arguments:
- tokens: bfloat16 [12288, 768], P('dp'), may hold values from -6 to 6
- grad_out: bfloat16 [12288, 768], P('dp'), may hold values from -8 to 8
- token_weight: float32 [12288], P('dp'), may hold values from 0.5 to 2
- lengths: int32 [24], P('dp'), may hold values from 1 to 512, 6144 in all
- step: int32 [1], replicated, may hold values from 2 to 20
- qkv_weight: bfloat16 [3, 768, 768], P(None, 'dp', 'tensor'), may hold values from -0.21875 to 0.21875
- out_weight: bfloat16 [768, 768], P('tensor', 'dp'), may hold values from -1.75 to 1.75
- up_weight: bfloat16 [768, 3072], P('dp', 'tensor'), may hold values from -0.21875 to 0.21875
- down_weight: bfloat16 [3072, 768], P('tensor', 'dp'), may hold values from -0.109375 to 0.109375
- norm_params: bfloat16 [4, 768], P(None, 'dp'), may hold values from 0.5 to 1.5
- first_qkv: float32 [3, 768, 768], P(None, 'dp', 'tensor'), may hold values from -32 to 32
- first_out: float32 [768, 768], P('tensor', 'dp'), may hold values from -4 to 4
- first_up: float32 [768, 3072], P('dp', 'tensor'), may hold values from -20 to 20
- first_down: float32 [3072, 768], P('tensor', 'dp'), may hold values from -40 to 40
- first_norm: float32 [4, 768], P(None, 'dp'), may hold values from -56 to 56
- second_qkv: float32 [3, 768, 768], P(None, 'dp', 'tensor'), may hold values from 143.21678 to 572.8671
- second_out: float32 [768, 768], P('tensor', 'dp'), may hold values from 2.2413425 to 8.951049
- second_up: float32 [768, 3072], P('dp', 'tensor'), may hold values from 57.01632 to 227.9424
- second_down: float32 [3072, 768], P('tensor', 'dp'), may hold values from 191.6928 to 768
- second_norm: float32 [4, 768], P(None, 'dp'), may hold values from 391.3728 to 1566.72
Outputs:
- output: bfloat16 [12288, 768], P('dp')
- grad_input: float32 [12288, 768], P('dp')
- new_qkv: float32 [3, 768, 768], P(None, 'dp', 'tensor')
- moment_qkv: float32 [3, 768, 768], P(None, 'dp', 'tensor')
- square_qkv: float32 [3, 768, 768], P(None, 'dp', 'tensor')
- copy_qkv: bfloat16 [3, 768, 768], P(None, 'dp', 'tensor')
- new_out: float32 [768, 768], P('tensor', 'dp')
- moment_out: float32 [768, 768], P('tensor', 'dp')
- square_out: float32 [768, 768], P('tensor', 'dp')
- copy_out: bfloat16 [768, 768], P('tensor', 'dp')
- new_up: float32 [768, 3072], P('dp', 'tensor')
- moment_up: float32 [768, 3072], P('dp', 'tensor')
- square_up: float32 [768, 3072], P('dp', 'tensor')
- copy_up: bfloat16 [768, 3072], P('dp', 'tensor')
- new_down: float32 [3072, 768], P('tensor', 'dp')
- moment_down: float32 [3072, 768], P('tensor', 'dp')
- square_down: float32 [3072, 768], P('tensor', 'dp')
- copy_down: bfloat16 [3072, 768], P('tensor', 'dp')
- new_norm: float32 [4, 768], P(None, 'dp')
- moment_norm: float32 [4, 768], P(None, 'dp')
- square_norm: float32 [4, 768], P(None, 'dp')
- copy_norm: bfloat16 [4, 768], P(None, 'dp')
Inputs may be any that keep to these rules, and one draw needn't show every extreme that they name: `lengths`: used tokens of each sequence; one sequence uses all 512 slots.
All inputs are finite; a program needn't handle non-finite values. No bound on the sum of `lengths` on one device may be relied on, other than what follows from the above.
Results may differ from a plain program's by a relative error of at most 0.014.
Values may be sent and summed in bfloat16 or wider, within the bound.
No kernel may reach another device: no remote copies, remote signals or barrier semaphores. Data moves between devices by JAX's collectives and lax.ppermute only.
A program may use at most 128 MiB of HBM per device.

v0:
```python
import jax
import jax.numpy as jnp
from jax import lax
from jax.sharding import PartitionSpec as P

HD = 64
NORM_EPS = 1e-05
BETA_ONE = 0.9
BETA_TWO = 0.95
ADAM_EPS = 1e-08
DECAY_RATE = 0.01
PEAK_RATE = 0.15
WARM_STEPS = 2.0
LAST_STEP = 40.0
MASK_VALUE = -1000000000.0


def exact_gelu(values):
    return jax.nn.gelu(values, approximate=False)


def norm_forward(summed, gain, shift):
    center = summed - jnp.mean(summed, axis=-1, keepdims=True)
    inverse = lax.rsqrt(jnp.mean(center * center, axis=-1, keepdims=True) + NORM_EPS)
    normed = center * inverse
    return (normed * gain + shift, normed, inverse)


def norm_backward(upstream, normed, inverse, gain):
    scaled = upstream * gain
    inner = (
        scaled
        - jnp.mean(scaled, axis=-1, keepdims=True)
        - normed * jnp.mean(scaled * normed, axis=-1, keepdims=True)
    )
    return (inner * inverse, jnp.sum(upstream * normed, axis=0), jnp.sum(upstream, axis=0))


def adamw_update(gradient, weight_low, first, second, rate, fix_one, fix_two, decay):
    weight = weight_low.astype(jnp.float32)
    first_new = BETA_ONE * first + (1.0 - BETA_ONE) * gradient
    second_new = BETA_TWO * second + (1.0 - BETA_TWO) * gradient * gradient
    direction = first_new / fix_one / (jnp.sqrt(second_new / fix_two) + ADAM_EPS)
    weight_new = weight - rate * (direction + decay * weight)
    return (weight_new, first_new, second_new, weight_new.astype(jnp.bfloat16))


def on_device(
    tokens,
    grad_out,
    token_weight,
    lengths,
    step,
    qkv_weight,
    out_weight,
    up_weight,
    down_weight,
    norm_params,
    first_qkv,
    first_out,
    first_up,
    first_down,
    first_norm,
    second_qkv,
    second_out,
    second_up,
    second_down,
    second_norm,
):
    qkv_full, out_full, up_full, down_full, norm_full = (
        lax.all_gather(qkv_weight, "dp", axis=1, tiled=True),
        lax.all_gather(out_weight, "dp", axis=1, tiled=True),
        lax.all_gather(up_weight, "dp", axis=0, tiled=True),
        lax.all_gather(down_weight, "dp", axis=1, tiled=True),
        lax.all_gather(norm_params, "dp", axis=1, tiled=True),
    )
    norm_float = norm_full.astype(jnp.float32)
    seq_count = lengths.shape[0]
    tok_count = tokens.shape[0]
    seq_len = tok_count // seq_count
    local_width = qkv_full.shape[2]
    local_heads = local_width // HD
    score_scale = HD ** (-0.5)
    tok_float = tokens.astype(jnp.float32)
    projected = jnp.einsum(
        "td,cde->cte", tokens, qkv_full, preferred_element_type=jnp.float32
    ).astype(jnp.bfloat16)
    split_heads = projected.reshape(3, seq_count, seq_len, local_heads, HD)
    queries, key_rows, value_rows = (split_heads[0], split_heads[1], split_heads[2])
    key_valid = jnp.arange(seq_len, dtype=jnp.int32)[None, :] < lengths[:, None]
    key_mask = key_valid[:, None, None, :]

    def attention_scores():
        raw_scores = jnp.einsum(
            "sqhe,skhe->shqk", queries, key_rows, preferred_element_type=jnp.float32
        )
        return jnp.where(key_mask, raw_scores * score_scale, MASK_VALUE)

    first_scores = attention_scores()
    log_total = jax.nn.logsumexp(first_scores, axis=-1, keepdims=True)
    probs_low = jnp.exp(first_scores - log_total).astype(jnp.bfloat16)
    context = jnp.einsum(
        "shqk,skhe->sqhe", probs_low, value_rows, preferred_element_type=jnp.float32
    )
    context_low = context.reshape(tok_count, local_width).astype(jnp.bfloat16)
    attn_part = jnp.dot(context_low, out_full, preferred_element_type=jnp.float32)
    attn_total = lax.psum(attn_part, "tensor")
    hidden_one, normed_one, inverse_one = norm_forward(
        tok_float + attn_total, norm_float[0], norm_float[1]
    )
    hidden_mine = hidden_one.astype(jnp.bfloat16)
    up_value = jnp.dot(hidden_mine, up_full, preferred_element_type=jnp.float32)
    gelu_value, gelu_pull = jax.vjp(exact_gelu, up_value)
    inner_low = gelu_value.astype(jnp.bfloat16)
    ffn_part = jnp.dot(inner_low, down_full, preferred_element_type=jnp.float32)
    ffn_total = lax.psum(ffn_part, "tensor")
    result, normed_two, inverse_two = norm_forward(
        hidden_one + ffn_total, norm_float[2], norm_float[3]
    )
    tok_valid = key_valid.reshape(tok_count).astype(jnp.float32)
    upstream = grad_out.astype(jnp.float32) * token_weight[:, None] * tok_valid[:, None]
    grad_two, gain_two, shift_two = norm_backward(upstream, normed_two, inverse_two, norm_float[2])
    ffn_mine = grad_two.astype(jnp.bfloat16)
    grad_down = jnp.einsum("tf,td->fd", inner_low, ffn_mine, preferred_element_type=jnp.float32)
    grad_inner = jnp.dot(ffn_mine, down_full.T, preferred_element_type=jnp.float32)
    up_low = gelu_pull(grad_inner)[0].astype(jnp.bfloat16)
    grad_up = jnp.einsum("td,tf->df", hidden_mine, up_low, preferred_element_type=jnp.float32)
    hidden_part = jnp.dot(up_low, up_full.T, preferred_element_type=jnp.float32)
    hidden_grad = grad_two + lax.psum(hidden_part, "tensor")
    grad_one, gain_one, shift_one = norm_backward(
        hidden_grad, normed_one, inverse_one, norm_float[0]
    )
    attn_mine = grad_one.astype(jnp.bfloat16)
    grad_outw = jnp.einsum("te,td->ed", context_low, attn_mine, preferred_element_type=jnp.float32)
    context_grad = jnp.dot(attn_mine, out_full.T, preferred_element_type=jnp.float32).astype(
        jnp.bfloat16
    )
    context_grad = context_grad.reshape(seq_count, seq_len, local_heads, HD)
    probs = jnp.exp(attention_scores() - log_total)
    probs_again = probs.astype(jnp.bfloat16)
    probs_grad = jnp.einsum(
        "sqhe,skhe->shqk", context_grad, value_rows, preferred_element_type=jnp.float32
    )
    value_grad = jnp.einsum(
        "shqk,sqhe->skhe", probs_again, context_grad, preferred_element_type=jnp.float32
    )
    score_grad = (
        probs * (probs_grad - jnp.sum(probs_grad * probs, axis=-1, keepdims=True)) * score_scale
    ).astype(jnp.bfloat16)
    query_grad = jnp.einsum(
        "shqk,skhe->sqhe", score_grad, key_rows, preferred_element_type=jnp.float32
    )
    key_grad = jnp.einsum(
        "shqk,sqhe->skhe", score_grad, queries, preferred_element_type=jnp.float32
    )
    proj_grad = (
        jnp.stack([query_grad, key_grad, value_grad])
        .astype(jnp.bfloat16)
        .reshape(3, tok_count, local_width)
    )
    grad_qkv = jnp.einsum("td,cte->cde", tokens, proj_grad, preferred_element_type=jnp.float32)
    input_part = jnp.einsum("cte,cde->td", proj_grad, qkv_full, preferred_element_type=jnp.float32)
    norm_partial = jnp.stack([gain_one, shift_one, gain_two, shift_two])
    result_low = result.astype(jnp.bfloat16)
    input_grad = grad_one + lax.psum(input_part, "tensor")
    shard_qkv, shard_out, shard_up, shard_down, shard_norm = (
        lax.psum_scatter(grad_qkv, "dp", scatter_dimension=1, tiled=True),
        lax.psum_scatter(grad_outw, "dp", scatter_dimension=1, tiled=True),
        lax.psum_scatter(grad_up, "dp", scatter_dimension=0, tiled=True),
        lax.psum_scatter(grad_down, "dp", scatter_dimension=1, tiled=True),
        lax.psum_scatter(norm_partial, "dp", scatter_dimension=1, tiled=True),
    )
    step_float = step[0].astype(jnp.float32)
    rate = PEAK_RATE * jnp.minimum(
        step_float / WARM_STEPS, (LAST_STEP - step_float) / (LAST_STEP - WARM_STEPS)
    )
    fix_one = 1.0 - BETA_ONE**step_float
    fix_two = 1.0 - BETA_TWO**step_float
    upd_qkv = adamw_update(
        shard_qkv, qkv_weight, first_qkv, second_qkv, rate, fix_one, fix_two, DECAY_RATE
    )
    upd_out = adamw_update(
        shard_out, out_weight, first_out, second_out, rate, fix_one, fix_two, DECAY_RATE
    )
    upd_up = adamw_update(
        shard_up, up_weight, first_up, second_up, rate, fix_one, fix_two, DECAY_RATE
    )
    upd_down = adamw_update(
        shard_down, down_weight, first_down, second_down, rate, fix_one, fix_two, DECAY_RATE
    )
    upd_norm = adamw_update(
        shard_norm, norm_params, first_norm, second_norm, rate, fix_one, fix_two, 0.0
    )
    return (
        result_low,
        input_grad,
        upd_qkv[0],
        upd_qkv[1],
        upd_qkv[2],
        upd_qkv[3],
        upd_out[0],
        upd_out[1],
        upd_out[2],
        upd_out[3],
        upd_up[0],
        upd_up[1],
        upd_up[2],
        upd_up[3],
        upd_down[0],
        upd_down[1],
        upd_down[2],
        upd_down[3],
        upd_norm[0],
        upd_norm[1],
        upd_norm[2],
        upd_norm[3],
    )


def solution(mesh):
    return jax.shard_map(
        on_device,
        mesh=mesh,
        in_specs=(
            P("dp", None),
            P("dp", None),
            P("dp"),
            P("dp"),
            P(),
            P(None, "dp", "tensor"),
            P("tensor", "dp"),
            P("dp", "tensor"),
            P("tensor", "dp"),
            P(None, "dp"),
            P(None, "dp", "tensor"),
            P("tensor", "dp"),
            P("dp", "tensor"),
            P("tensor", "dp"),
            P(None, "dp"),
            P(None, "dp", "tensor"),
            P("tensor", "dp"),
            P("dp", "tensor"),
            P("tensor", "dp"),
            P(None, "dp"),
        ),
        out_specs=(
            P("dp", None),
            P("dp", None),
            P(None, "dp", "tensor"),
            P(None, "dp", "tensor"),
            P(None, "dp", "tensor"),
            P(None, "dp", "tensor"),
            P("tensor", "dp"),
            P("tensor", "dp"),
            P("tensor", "dp"),
            P("tensor", "dp"),
            P("dp", "tensor"),
            P("dp", "tensor"),
            P("dp", "tensor"),
            P("dp", "tensor"),
            P("tensor", "dp"),
            P("tensor", "dp"),
            P("tensor", "dp"),
            P("tensor", "dp"),
            P(None, "dp"),
            P(None, "dp"),
            P(None, "dp"),
            P(None, "dp"),
        ),
        check_vma=False,
    )
```

profile of v0, /device:TPU:0, one launch (start us, length us, event | category | flops | bytes accessed | tf_op | source)
XLA Modules:
  0.0 818.7 jit_solution(9086663741849592017)
XLA Ops:
  8.8 1.0 copy.117
  9.8 38.8 %all_gather.15 = bf16[3,768,192]{2,0,1:T(4,128)(2,1)S(1)} all-gather(bf16[3,96,192]{2,0,1:T(4,128)(2,1)S(1)} %copy.117), channel_id=1, replica_groups=mesh['dp'=8,'tensor'=4] {'dp'}, dimensions={1}, use_global_device_ids=true | all-gather | bytes 995328 | tf_op jit(solution)/shard_map/all_gather | solution.py:71
  48.6 4.4 fusion.39
  54.1 2.4 fusion.2
  56.5 2.2 exponential_reduce_fusion
  58.7 1.4 copy-done.2
  60.6 5.3 fusion.58
  66.7 31.2 %all_gather.16 = bf16[192,768]{0,1:T(8,128)(2,1)S(1)} all-gather(bf16[192,96]{0,1:T(8,128)(2,1)S(1)} %copy.124), channel_id=1, replica_groups=mesh['dp'=8,'tensor'=4] {'dp'}, dimensions={1}, use_global_device_ids=true | all-gather | bytes 331776 | tf_op jit(solution)/shard_map/all_gather | solution.py:72
  97.9 3.0 fusion.127
  102.2 18.7 %all-gather = bf16[8,96,4]{1,2,0:T(4,128)(2,1)S(1)} all-gather(bf16[1,96,4]{1,2,0:T(4,128)(2,1)S(1)} %bitcast.84), channel_id=1, replica_groups=mesh['dp'=8,'tensor'=4] {'dp'}, dimensions={0}, use_global_device_ids=true | all-gather | bytes 6912 | tf_op jit(solution)/shard_map/all_gather | solution.py:75
  121.0 73.1 %all-reduce.5.cloned.1.call-done = f32[1536,768]{1,0:T(8,128)} async-done(((f32[1536,768]{1,0:T(8,128)}), f32[1536,768]{1,0:T(8,128)}) %all-reduce.5.cloned.1.call-update) | async-done | bytes 4718608 | tf_op jit(solution)/shard_map/psum | solution.py:107
  194.2 2.9 fusion.125
  197.8 1.5 copy-done
  199.3 1.1 fusion.38
  200.4 14.3 %multiply_convert_fusion.1 = (bf16[1536,768]{1,0:T(8,128)(2,1)}, f32[1536,768]{1,0:T(8,128)}, f32[1536,768]{1,0:T(8,128)}) fusion(bf16[1536,768]{1,0:T(8,128)(2,1)S(1)} %fusion.38, bf16[768,768]{1,0:T(8,128)(2,1)} %all-gather.4.cloned.1.call-done), kind=kOutput, calls=%fused_computation.26 | convolution fusion | flops 1888616448 | bytes 15335424 | tf_op jit(solution)/shard_map/dot_general | solution.py:112
  214.7 6.3 fusion.128
  221.2 94.1 %all-reduce.7.cloned.1.call-done = f32[1536,768]{1,0:T(8,128)} async-done(((f32[1536,768]{1,0:T(8,128)}), f32[1536,768]{1,0:T(8,128)}) %all-reduce.7.cloned.1.call-update) | async-done | bytes 4718608 | tf_op jit(solution)/shard_map/psum | solution.py:116
  315.3 4.7 fusion.122
  320.7 0.9 copy-done.4
  321.6 2.9 multiply_reduce_fusion.1
  324.6 4.4 subtract_multiply_fusion.1
  329.1 3.3 add_convert_fusion
  332.4 1.4 copy-done.11
  333.9 4.3 fusion.129
  339.7 92.9 %all-reduce.9.cloned.1.call-done = f32[1536,768]{1,0:T(8,128)} async-done(((f32[1536,768]{1,0:T(8,128)}), f32[1536,768]{1,0:T(8,128)}) %all-reduce.9.cloned.1.call-update) | async-done | bytes 4718608 | tf_op jit(solution)/shard_map/psum | solution.py:129
  432.5 7.1 multiply_reduce_fusion.2
  439.6 3.3 subtract_multiply_fusion
  443.0 2.2 copy-done.1
  445.2 1.8 convolution_convert_fusion.1
  446.9 2.2 reshape.173
  449.1 7.2 fusion.59
  456.3 5.1 fusion.71
  461.4 1.9 convolution_bitcast_fusion.1
  464.8 1.0 copy.153
  466.3 18.4 %fusion.52 = bf16[3,512,3,64]{1,3,2,0:T(8,128)(2,1)} fusion(f32[3,3,512,512]{2,3,1,0:T(8,128)} %fusion.71, f32[3,3,512,512]{2,3,1,0:T(8,128)} %copy-done.2, f32[3,3,512]{2,1,0:T(4,128)S(1)} %copy-done.26, pred[3,512]{1,0:T(4,128)(4,1)S(1)} %get-tuple-element.155, bf16[3,512,3,64]{1,0,3,2:T(4,128)(2,1)} %copy-done.6), kind=kOutput, calls=%fused_computation.69 | convolution fusion | flops 328242176 | bytes 20073984 | tf_op jit(solution)/shard_map/shqk,sqhe->skhe/dot_general | solution.py:153
  484.7 18.3 %fusion.55 = bf16[3,512,3,64]{1,3,2,0:T(8,128)(2,1)} fusion(f32[3,3,512,512]{2,3,1,0:T(8,128)} %fusion.71, f32[3,3,512,512]{2,3,1,0:T(8,128)} %copy-done.2, f32[3,3,512]{2,1,0:T(4,128)S(1)} %copy-done.26, pred[3,512]{1,0:T(4,128)(4,1)S(1)} %get-tuple-element.155, bf16[3,512,3,64]{1,0,3,2:T(4,128)(2,1)} %copy-done.5), kind=kOutput, calls=%fused_computation.70 | convolution fusion | flops 328242176 | bytes 20073984 | tf_op jit(solution)/shard_map/shqk,skhe->sqhe/dot_general | solution.py:150
  503.0 1.4 copy.136
  504.4 2.0 stack.29
  506.3 2.5 copy.133
  508.8 2.5 stack.28
  511.3 2.5 copy.130
  513.8 2.5 stack.27
  516.4 1.1 constant_dynamic-update-slice_fusion.2
  517.5 1.1 constant_dynamic-update-slice_fusion.1
  518.7 1.3 copy-done.22
  520.0 5.6 convolution_bitcast_fusion
  525.7 6.5 fusion.62
  532.3 5.1 fusion.130
  537.5 5.0 fusion.43
  542.5 3.2 copy.149
  545.8 2.8 reshape.182
  549.5 1.1 copy.139
  550.6 1.1 copy.140
  553.3 39.2 %reduce-scatter.18.cloned.1.call-done = f32[96,192]{1,0:T(8,128)} async-done(((f32[768,192]{1,0:T(8,128)}), f32[96,192]{1,0:T(8,128)}) %reduce-scatter.18.cloned.1.call-update) | async-done | bytes 73744
  592.5 1.0 copy.152
  593.5 1.7 fusion.118
  595.2 24.7 %all-reduce.11.cloned.1.call-done = f32[1536,768]{1,0:T(8,128)} async-done(((f32[1536,768]{1,0:T(8,128)}), f32[1536,768]{1,0:T(8,128)}) %all-reduce.11.cloned.1.call-update) | async-done | bytes 4718608 | tf_op jit(solution)/shard_map/psum | solution.py:165
  619.9 6.6 add.161
  626.6 38.0 %reduce-scatter.14.cloned.1.call-done = f32[768,96]{0,1:T(8,128)} async-done(((f32[768,768]{0,1:T(8,128)}), f32[768,96]{0,1:T(8,128)}) %reduce-scatter.14.cloned.1.call-update) | async-done | bytes 294928 | tf_op jit(solution)/shard_map/reduce_scatter | solution.py:170
  664.5 2.1 fusion.114
  666.6 69.9 %reduce-scatter.12.cloned.1.call-done = f32[96,768]{1,0:T(8,128)} async-done(((f32[768,768]{1,0:T(8,128)}), f32[96,768]{1,0:T(8,128)}) %reduce-scatter.12.cloned.1.call-update) | async-done | bytes 294928 | tf_op jit(solution)/shard_map/reduce_scatter | solution.py:169
  736.5 2.1 fusion.116
  738.6 67.8 %reduce-scatter.16.cloned.1.call-done = f32[96,576]{1,0:T(8,128)} async-done(((f32[768,576]{1,0:T(8,128)}), f32[96,576]{1,0:T(8,128)}) %reduce-scatter.16.cloned.1.call-update) | async-done | bytes 221200
  806.4 1.1 reshape.183
  (140 shorter events, 15.4 us)
Async XLA Ops:
  8.0 186.1 %all-reduce.5.cloned.1.call-start = ((), (), s32[]{:S(2)}) async-start(), calls=%async_computation.5 | async-start | bytes 9437184 | tf_op jit(solution)/shard_map/psum | solution.py:107
  48.6 4.4 copy-start.12
  53.6 2.8 copy-start.6
  54.1 2.4 copy-start.5
  56.5 3.6 copy-start.2
  60.1 5.8 copy-start.25
  60.6 5.3 copy-start.7
  60.6 6.0 copy-start.21
  97.9 4.3 copy-start.28
  97.9 96.3 %copy-start.10 = (bf16[1536,768]{1,0:T(8,128)(2,1)S(1)}, bf16[1536,768]{1,0:T(8,128)(2,1)}, u32[]{:S(2)}) copy-start(bf16[1536,768]{1,0:T(8,128)(2,1)} %param.20) | copy-start | bytes 7077892
  101.0 99.4 %all-gather.4.cloned.1.call-start = ((), (), s32[]{:S(2)}) async-start(), calls=%async_computation.6 | async-start | bytes 1327104 | tf_op jit(solution)/shard_map/all_gather | solution.py:73
  101.5 113.1 %all-gather.6.cloned.1.call-start = ((), (), s32[]{:S(2)}) async-start(), calls=%async_computation.7 | async-start | bytes 1327104 | tf_op jit(solution)/shard_map/all_gather | solution.py:74
  102.1 213.2 %all-reduce.7.cloned.1.call-start = ((), (), s32[]{:S(2)}) async-start(), calls=%async_computation.8 | async-start | bytes 9437184 | tf_op jit(solution)/shard_map/psum | solution.py:116
  197.0 2.2 copy-start
  221.0 211.6 %all-reduce.9.cloned.1.call-start = ((), (), s32[]{:S(2)}) async-start(), calls=%async_computation.9 | async-start | bytes 9437184 | tf_op jit(solution)/shard_map/psum | solution.py:129
  319.9 1.7 copy-start.4
  320.0 1.7 copy-start.24
  321.6 7.4 slice-start.2
  321.6 7.4 slice-start.4
  324.6 4.5 copy-start.33
  324.6 4.5 slice-start.3
  324.6 4.5 slice-start.5
  329.0 3.4 copy-start.3
  329.1 4.8 copy-start.32
  332.4 1.5 copy-start.11
  338.2 213.6 %reduce-scatter.20.cloned.1.call-start = ((), (), s32[]{:S(2)}) async-start(), calls=%async_computation.15 | async-start | bytes 442368
  443.0 2.2 copy-start.1
  445.2 4.0 copy-start.26
  446.9 14.5 %slice-start = ((s8[4718592]{0:T(1024)(128)(4,1)}), s8[524288]{0:T(1024)(128)(4,1)S(1)}, s32[]{:S(2)}) async-start(s8[4718592]{0:T(1024)(128)(4,1)} %bitcast.73), calls=%async_computation.16 | async-start | bytes 1048576
  449.1 7.2 copy-start.8
  449.1 7.2 copy-start.9
  449.1 12.3 %slice-start.1 = ((s8[4718592]{0:T(1024)(128)(4,1)}), s8[4194304]{0:T(1024)(128)(4,1)S(1)}, s32[]{:S(2)}) async-start(s8[4718592]{0:T(1024)(128)(4,1)} %bitcast.73), calls=%async_computation.17 | async-start | bytes 8388608
  461.4 2.6 copy-start.27
  465.8 126.8 %reduce-scatter.18.cloned.1.call-start = ((), (), s32[]{:S(2)}) async-start(), calls=%async_computation.14 | async-start | bytes 884736
  484.7 18.3 %copy-start.16 = (bf16[3,512,3,64]{1,3,2,0:T(8,128)(2,1)S(1)}, bf16[3,512,3,64]{1,3,2,0:T(8,128)(2,1)}, u32[]{:S(2)}) copy-start(bf16[3,512,3,64]{1,3,2,0:T(8,128)(2,1)} %fusion.59) | copy-start | bytes 1769476
  516.3 103.6 %all-reduce.11.cloned.1.call-start = ((), (), s32[]{:S(2)}) async-start(), calls=%async_computation.10 | async-start | bytes 9437184 | tf_op jit(solution)/shard_map/psum | solution.py:165
  518.7 1.3 copy-start.22
  525.6 138.9 %reduce-scatter.14.cloned.1.call-start = ((), (), s32[]{:S(2)}) async-start(), calls=%async_computation.12 | async-start | bytes 2654208 | tf_op jit(solution)/shard_map/reduce_scatter | solution.py:170
  532.2 204.3 %reduce-scatter.12.cloned.1.call-start = ((), (), s32[]{:S(2)}) async-start(), calls=%async_computation.11 | async-start | bytes 2654208 | tf_op jit(solution)/shard_map/reduce_scatter | solution.py:169
  537.4 268.9 %reduce-scatter.16.cloned.1.call-start = ((), (), s32[]{:S(2)}) async-start(), calls=%async_computation.13 | async-start | bytes 2211840
  545.7 2.9 copy-start.15
  545.7 7.0 copy-start.29
  545.7 7.0 copy-start.30
  545.7 7.0 copy-start.31
  545.8 47.8 %copy-start.23 = (f32[192,96]{1,0:T(8,128)S(1)}, f32[192,96]{1,0:T(8,128)}, u32[]{:S(2)}) copy-start(f32[192,96]{1,0:T(8,128)} %param.36) | copy-start | bytes 221188
  595.2 69.4 %copy-start.13 = (bf16[768,96]{0,1:T(8,128)(2,1)S(1)}, bf16[768,96]{0,1:T(8,128)(2,1)}, u32[]{:S(2)}) copy-start(bf16[768,96]{0,1:T(8,128)(2,1)} %param.28) | copy-start | bytes 442372
  595.2 69.4 %copy-start.17 = (f32[768,96]{0,1:T(8,128)S(1)}, f32[768,96]{0,1:T(8,128)}, u32[]{:S(2)}) copy-start(f32[768,96]{0,1:T(8,128)} %param.38) | copy-start | bytes 884740
  595.2 69.4 %copy-start.18 = (f32[768,96]{0,1:T(8,128)S(1)}, f32[768,96]{0,1:T(8,128)}, u32[]{:S(2)}) copy-start(f32[768,96]{0,1:T(8,128)} %param.33) | copy-start | bytes 884740
  595.2 141.3 %copy-start.14 = (bf16[96,768]{1,0:T(8,128)(2,1)S(1)}, bf16[96,768]{1,0:T(8,128)(2,1)}, u32[]{:S(2)}) copy-start(bf16[96,768]{1,0:T(8,128)(2,1)} %param.27) | copy-start | bytes 442372
  595.2 141.3 %copy-start.19 = (f32[96,768]{1,0:T(8,128)S(1)}, f32[96,768]{1,0:T(8,128)}, u32[]{:S(2)}) copy-start(f32[96,768]{1,0:T(8,128)} %param.37) | copy-start | bytes 884740
  595.2 141.3 %copy-start.20 = (f32[96,768]{1,0:T(8,128)S(1)}, f32[96,768]{1,0:T(8,128)}, u32[]{:S(2)}) copy-start(f32[96,768]{1,0:T(8,128)} %param.32) | copy-start | bytes 884740
Sparse Core Ops, SparseCore 0:
  101.1 93.0 all-reduce.4
  221.1 94.1 all-reduce.6
  338.3 94.1 all-reduce.8
  525.8 94.1 all-reduce.10
Sparse Core Ops, SparseCore 1:
  103.6 40.4 all-gather.3
  146.2 40.0 all-gather.5
  465.8 61.6 reduce-scatter.19
  530.8 61.6 reduce-scatter.17
  596.4 68.0 reduce-scatter.13
  668.4 68.0 reduce-scatter.11
  740.3 66.0 reduce-scatter.15
where the time goes:
time: 826 us; the launch traced here: 819 us
  waiting for transfers between devices  501 us (61%)
  matrix products  118 us (14%)
  blocking collectives  88.7 us (11%)
  local copies, waits for them, and re-layouts  47.8 us (6%)
  other arithmetic  44.7 us (5%)
  between operations  16.9 us (2%)
    unnamed x14, waiting for transfers between devices  108 us
    psum x1, waiting for transfers between devices, on_device(): ffn_total = lax.psum(ffn_part, 'tensor')  94.1 us
    psum x1, waiting for transfers between devices, on_device(): hidden_grad = grad_two + lax.psum(hidden_part, 'tensor')  92.9 us
    psum x1, waiting for transfers between devices, on_device(): attn_total = lax.psum(attn_part, 'tensor')  73.1 us
    reduce_scatter x1, waiting for transfers between devices, on_device(): lax.psum_scatter(grad_up, 'dp', scatter_dimension=0, tiled=True)  69.9 us
    all_gather x1, blocking collectives, on_device(): lax.all_gather(qkv_weight, 'dp', axis=1, tiled=True)  38.8 us
    reduce_scatter x1, waiting for transfers between devices, on_device(): lax.psum_scatter(grad_down, 'dp', scatter_dimension=1, tiled=True)  38 us
    all_gather x1, blocking collectives, on_device(): lax.all_gather(out_weight, 'dp', axis=1, tiled=True)  31.2 us
  transfers between devices with their start and end apart: 11, of which 8 were waited for; matrix products, arithmetic and copies ran while one was open for 14% of the time, Pallas kernels for 0%

commit v1 on v0

--- a/solution.py
+++ b/solution.py
@@ -2,6 +2,7 @@
 import jax.numpy as jnp
 from jax import lax
 from jax.sharding import PartitionSpec as P
+from jax.lax import all_gather
 
 HD = 64
 NORM_EPS = 1e-05
@@ -104,7 +105,8 @@
     )
     context_low = context.reshape(tok_count, local_width).astype(jnp.bfloat16)
     attn_part = jnp.dot(context_low, out_full, preferred_element_type=jnp.float32)
-    attn_total = lax.psum(attn_part, "tensor")
+    m_next = all_gather(attn_part, axis_name="tensor")
+    attn_total = jnp.sum(m_next, 0)
     hidden_one, normed_one, inverse_one = norm_forward(
         tok_float + attn_total, norm_float[0], norm_float[1]
     )

time: 826 us -> 985 us (1.19)
  waiting for transfers between devices: 501 us -> 666 us
  local copies, waits for them, and re-layouts: 47.8 us -> 35 us
  other arithmetic: 44.7 us -> 56.6 us
    all_gather x0 -> x1, waiting for transfers between devices: none -> 98.8 us  [on_device(): m_next = all_gather(attn_part, axis_name='tensor')]
    psum x1 -> x0, waiting for transfers between devices: 73.1 us -> none  [on_device(): attn_total = lax.psum(attn_part, 'tensor')]
    psum x1, waiting for transfers between devices: 24.7 us -> 93.4 us  [on_device(): input_grad = grad_one + lax.psum(input_part, 'tensor')]
    reduce_scatter x1, waiting for transfers between devices: 38 us -> 69.1 us  [on_device(): lax.psum_scatter(grad_down, 'dp', scatter_dimension=1, tiled=True)]
    all_gather x1, waiting for transfers between devices: 0.01 us -> 27.8 us  [on_device(): lax.all_gather(down_weight, 'dp', axis=1, tiled=True)]
    all_gather x1, waiting for transfers between devices: 0.03 us -> 26.6 us  [on_device(): lax.all_gather(up_weight, 'dp', axis=0, tiled=True)]
    unnamed x14, waiting for transfers between devices: 108 us -> 93.7 us
    reduce_sum x0 -> x1, other arithmetic: none -> 10.6 us  [on_device(): attn_total = jnp.sum(m_next, 0)]
  transfers between devices with their start and end apart: 11 -> 11, of which waited for: 8 -> 10; matrix products, arithmetic and copies ran while one was open for 14% -> 14% of each run, Pallas kernels for 0% -> 0%
where the time goes in v1:
time: 985 us; the launch traced here: 978 us
  waiting for transfers between devices  666 us (68%)
  matrix products  115 us (12%)
  blocking collectives  88.7 us (9%)
  other arithmetic  56.6 us (6%)
  local copies, waits for them, and re-layouts  35 us (4%)
  between operations  15.5 us (2%)
    all_gather x1, waiting for transfers between devices, on_device(): m_next = all_gather(attn_part, axis_name='tensor')  98.8 us
    psum x1, waiting for transfers between devices, on_device(): hidden_grad = grad_two + lax.psum(hidden_part, 'tensor')  94.3 us
    unnamed x14, waiting for transfers between devices  93.7 us
    psum x1, waiting for transfers between devices, on_device(): input_grad = grad_one + lax.psum(input_part, 'tensor')  93.4 us
    psum x1, waiting for transfers between devices, on_device(): ffn_total = lax.psum(ffn_part, 'tensor')  92.7 us
    reduce_scatter x1, waiting for transfers between devices, on_device(): lax.psum_scatter(grad_up, 'dp', scatter_dimension=0, tiled=True)  69.9 us
    reduce_scatter x1, waiting for transfers between devices, on_device(): lax.psum_scatter(grad_down, 'dp', scatter_dimension=1, tiled=True)  69.1 us
    all_gather x1, blocking collectives, on_device(): lax.all_gather(qkv_weight, 'dp', axis=1, tiled=True)  38.8 us
  transfers between devices with their start and end apart: 11, of which 10 were waited for; matrix products, arithmetic and copies ran while one was open for 14% of the time, Pallas kernels for 0%

profile of v1, /device:TPU:0, one launch (start us, length us, event | category | flops | bytes accessed | tf_op | source)
XLA Modules:
  0.0 978.1 jit_solution(5528566863963331126)
XLA Ops:
  8.0 1.0 copy.117
  9.0 38.8 %all_gather.21 = bf16[3,768,192]{2,0,1:T(4,128)(2,1)S(1)} all-gather(bf16[3,96,192]{2,0,1:T(4,128)(2,1)S(1)} %copy.117), channel_id=1, replica_groups=mesh['dp'=8,'tensor'=4] {'dp'}, dimensions={1}, use_global_device_ids=true | all-gather | bytes 995328 | tf_op jit(solution)/shard_map/all_gather | solution.py:72
  47.8 4.4 fusion.39
  53.2 2.4 fusion.2
  55.7 2.2 exponential_reduce_fusion
  57.9 1.5 copy-done.2
  59.9 5.3 fusion.58
  66.0 31.2 %all_gather.22 = bf16[192,768]{0,1:T(8,128)(2,1)S(1)} all-gather(bf16[192,96]{0,1:T(8,128)(2,1)S(1)} %copy.124), channel_id=1, replica_groups=mesh['dp'=8,'tensor'=4] {'dp'}, dimensions={1}, use_global_device_ids=true | all-gather | bytes 331776 | tf_op jit(solution)/shard_map/all_gather | solution.py:73
  97.2 3.0 fusion.127
  101.8 18.7 %all-gather.1 = bf16[8,96,4]{1,2,0:T(4,128)(2,1)S(1)} all-gather(bf16[1,96,4]{1,2,0:T(4,128)(2,1)S(1)} %bitcast.84), channel_id=1, replica_groups=mesh['dp'=8,'tensor'=4] {'dp'}, dimensions={0}, use_global_device_ids=true | all-gather | bytes 6912 | tf_op jit(solution)/shard_map/all_gather | solution.py:76
  120.6 98.8 %all-gather.10.cloned.1.call-done = f32[6144,768]{1,0:T(8,128)} async-done(((f32[1536,768]{1,0:T(8,128)}), f32[6144,768]{1,0:T(8,128)}) %all-gather.10.cloned.1.call-update) | async-done | bytes 18874384 | tf_op jit(solution)/shard_map/all_gather | solution.py:108
  219.4 10.6 %reduce_sum.136 = f32[1536,768]{1,0:T(8,128)} reduce(f32[4,1536,768]{2,1,0:T(8,128)} %bitcast.74, f32[]{:T(128)} %constant.52.clone.1), dimensions={0}, to_apply=%region_2.3 | reduce | flops 3538944 | bytes 23592964 | tf_op jit(solution)/shard_map/reduce_sum | solution.py:109
  229.9 2.9 fusion.125
  233.5 1.4 copy-done
  234.9 1.1 fusion.38
  236.0 26.6 %all-gather.6.cloned.1.call-done = bf16[768,768]{1,0:T(8,128)(2,1)} async-done(((bf16[96,768]{1,0:T(8,128)(2,1)}), bf16[768,768]{1,0:T(8,128)(2,1)}) %all-gather.6.cloned.1.call-update) | async-done | bytes 1179664 | tf_op jit(solution)/shard_map/all_gather | solution.py:74
  262.6 14.3 %multiply_convert_fusion.1 = (bf16[1536,768]{1,0:T(8,128)(2,1)}, f32[1536,768]{1,0:T(8,128)}, f32[1536,768]{1,0:T(8,128)}) fusion(bf16[1536,768]{1,0:T(8,128)(2,1)S(1)} %fusion.38, bf16[768,768]{1,0:T(8,128)(2,1)} %all-gather.6.cloned.1.call-done), kind=kOutput, calls=%fused_computation.26 | convolution fusion | flops 1888616448 | bytes 15335424 | tf_op jit(solution)/shard_map/dot_general | solution.py:114
  276.9 27.8 %all-gather.8.cloned.1.call-done = bf16[768,768]{0,1:T(8,128)(2,1)} async-done(((bf16[768,96]{0,1:T(8,128)(2,1)}), bf16[768,768]{0,1:T(8,128)(2,1)}) %all-gather.8.cloned.1.call-update) | async-done | bytes 1179664 | tf_op jit(solution)/shard_map/all_gather | solution.py:75
  304.7 6.1 fusion.128
  311.1 92.7 %all-reduce.4.cloned.1.call-done = f32[1536,768]{1,0:T(8,128)} async-done(((f32[1536,768]{1,0:T(8,128)}), f32[1536,768]{1,0:T(8,128)}) %all-reduce.4.cloned.1.call-update) | async-done | bytes 4718608 | tf_op jit(solution)/shard_map/psum | solution.py:118
  403.8 4.7 fusion.122
  409.2 0.9 copy-done.4
  410.1 2.9 multiply_reduce_fusion.1
  413.1 4.4 subtract_multiply_fusion.1
  417.6 3.3 add_convert_fusion
  420.9 1.4 copy-done.13
  422.3 4.3 fusion.129
  426.7 94.3 %all-reduce.6.cloned.1.call-done = f32[1536,768]{1,0:T(8,128)} async-done(((f32[1536,768]{1,0:T(8,128)}), f32[1536,768]{1,0:T(8,128)}) %all-reduce.6.cloned.1.call-update) | async-done | bytes 4718608 | tf_op jit(solution)/shard_map/psum | solution.py:131
  521.0 7.7 multiply_reduce_fusion.2
  528.7 0.9 copy.153
  529.7 4.6 subtract_multiply_fusion
  534.4 2.2 copy-done.1
  536.5 2.0 convolution_bitcast_fusion.1
  538.6 6.5 fusion.62
  545.2 5.2 fusion.130
  550.9 3.3 convolution_convert_fusion.1
  554.6 6.1 fusion.59
  562.1 5.1 fusion.71
  567.1 16.9 %fusion.52 = bf16[3,512,3,64]{1,3,2,0:T(8,128)(2,1)S(1)} fusion(f32[3,3,512,512]{2,3,1,0:T(8,128)} %fusion.71, f32[3,3,512,512]{2,3,1,0:T(8,128)} %copy-done.2, f32[3,3,512]{2,1,0:T(4,128)S(1)} %log_add_fusion, pred[3,512]{1,0:T(4,128)(4,1)S(1)} %get-tuple-element.155, bf16[3,512,3,64]{1,0,3,2:T(4,128)(2,1)S(1)} %copy-done.8), kind=kOutput, calls=%fused_computation.69 | convolution fusion | flops 328242176 | bytes 20073984 | tf_op jit(solution)/shard_map/shqk,sqhe->skhe/dot_general | solution.py:155
  585.5 16.9 %fusion.55 = bf16[3,512,3,64]{1,3,2,0:T(8,128)(2,1)S(1)} fusion(f32[3,3,512,512]{2,3,1,0:T(8,128)} %fusion.71, f32[3,3,512,512]{2,3,1,0:T(8,128)} %copy-done.2, f32[3,3,512]{2,1,0:T(4,128)} %copy-done.23, pred[3,512]{1,0:T(4,128)(4,1)S(1)} %get-tuple-element.155, bf16[3,512,3,64]{1,0,3,2:T(4,128)(2,1)S(1)} %copy-done.6), kind=kOutput, calls=%fused_computation.70 | convolution fusion | flops 328242176 | bytes 20073984 | tf_op jit(solution)/shard_map/shqk,skhe->sqhe/dot_general | solution.py:152
  602.9 1.0 stack.27
  604.0 1.2 copy-done.21
  605.2 5.6 convolution_bitcast_fusion
  610.9 1.6 copy-done.12
  612.5 4.2 fusion.43
  616.8 3.0 copy.149
  619.8 2.8 reshape.183
  622.6 1.1 copy.138
  624.5 1.1 copy.139
  625.6 1.1 copy.140
  628.3 28.0 %reduce-scatter.18.cloned.1.call-done = f32[96,192]{1,0:T(8,128)} async-done(((f32[768,192]{1,0:T(8,128)}), f32[96,192]{1,0:T(8,128)}) %reduce-scatter.18.cloned.1.call-update) | async-done | bytes 73744
  656.3 1.0 copy.152
  657.3 1.7 fusion.118
  659.0 69.1 %reduce-scatter.14.cloned.1.call-done = f32[768,96]{0,1:T(8,128)} async-done(((f32[768,768]{0,1:T(8,128)}), f32[768,96]{0,1:T(8,128)}) %reduce-scatter.14.cloned.1.call-update) | async-done | bytes 294928 | tf_op jit(solution)/shard_map/reduce_scatter | solution.py:172
  728.1 2.2 fusion.114
  730.3 69.9 %reduce-scatter.12.cloned.1.call-done = f32[96,768]{1,0:T(8,128)} async-done(((f32[768,768]{1,0:T(8,128)}), f32[96,768]{1,0:T(8,128)}) %reduce-scatter.12.cloned.1.call-update) | async-done | bytes 294928 | tf_op jit(solution)/shard_map/reduce_scatter | solution.py:171
  800.2 2.1 fusion.116
  802.3 93.4 %all-reduce.8.cloned.1.call-done = f32[1536,768]{1,0:T(8,128)} async-done(((f32[1536,768]{1,0:T(8,128)}), f32[1536,768]{1,0:T(8,128)}) %all-reduce.8.cloned.1.call-update) | async-done | bytes 4718608 | tf_op jit(solution)/shard_map/psum | solution.py:167
  895.7 6.6 add.159
  902.3 64.2 %reduce-scatter.16.cloned.1.call-done = f32[96,576]{1,0:T(8,128)} async-done(((f32[768,576]{1,0:T(8,128)}), f32[96,576]{1,0:T(8,128)}) %reduce-scatter.16.cloned.1.call-update) | async-done | bytes 221200
  966.4 1.1 reshape.184
  968.0 0.9 copy.141
  968.9 0.9 copy.142
  969.7 0.9 copy.143
  (126 shorter events, 13.7 us)
Async XLA Ops:
  7.2 212.2 %all-gather.10.cloned.1.call-start = ((), (), s32[]{:S(2)}) async-start(), calls=%async_computation.12 | async-start | bytes 23592960 | tf_op jit(solution)/shard_map/all_gather | solution.py:108
  47.8 4.4 copy-start.14
  52.8 2.8 copy-start.7
  53.2 2.4 copy-start.5
  55.6 3.7 copy-start.2
  59.4 507.8 %copy-start.23 = (f32[3,3,512]{2,1,0:T(4,128)}, f32[3,3,512]{2,1,0:T(4,128)S(1)}, u32[]{:S(2)}) copy-start(f32[3,3,512]{2,1,0:T(4,128)S(1)} %log_add_fusion) | copy-start | bytes 55300
  59.8 5.3 copy-start.9
  59.8 6.0 copy-start.19
  97.2 4.6 copy-start.24
  100.2 162.4 %all-gather.6.cloned.1.call-start = ((), (), s32[]{:S(2)}) async-start(), calls=%async_computation.5 | async-start | bytes 1327104 | tf_op jit(solution)/shard_map/all_gather | solution.py:74
  101.0 203.7 %all-gather.8.cloned.1.call-start = ((), (), s32[]{:S(2)}) async-start(), calls=%async_computation.6 | async-start | bytes 1327104 | tf_op jit(solution)/shard_map/all_gather | solution.py:75
  101.7 302.1 %all-reduce.4.cloned.1.call-start = ((), (), s32[]{:S(2)}) async-start(), calls=%async_computation.7 | async-start | bytes 9437184 | tf_op jit(solution)/shard_map/psum | solution.py:118
  219.4 10.6 %copy-start.11 = (bf16[1536,768]{1,0:T(8,128)(2,1)S(1)}, bf16[1536,768]{1,0:T(8,128)(2,1)}, u32[]{:S(2)}) copy-start(bf16[1536,768]{1,0:T(8,128)(2,1)} %param.20) | copy-start | bytes 7077892
  232.8 2.1 copy-start
  310.9 210.1 %all-reduce.6.cloned.1.call-start = ((), (), s32[]{:S(2)}) async-start(), calls=%async_computation.8 | async-start | bytes 9437184 | tf_op jit(solution)/shard_map/psum | solution.py:131
  408.5 1.7 copy-start.4
  408.5 1.7 copy-start.22
  410.1 7.4 slice-start
  410.1 7.4 slice-start.2
  413.1 4.5 copy-start.28
  413.1 4.5 slice-start.1
  413.1 4.5 slice-start.3
  417.5 3.4 copy-start.3
  417.6 4.7 copy-start.27
  420.9 1.4 copy-start.13
  426.6 200.1 %reduce-scatter.20.cloned.1.call-start = ((), (), s32[]{:S(2)}) async-start(), calls=%async_computation.15 | async-start | bytes 442368
  529.7 126.6 %reduce-scatter.18.cloned.1.call-start = ((), (), s32[]{:S(2)}) async-start(), calls=%async_computation.14 | async-start | bytes 884736
  534.3 2.2 copy-start.1
  538.5 189.6 %reduce-scatter.14.cloned.1.call-start = ((), (), s32[]{:S(2)}) async-start(), calls=%async_computation.11 | async-start | bytes 2654208 | tf_op jit(solution)/shard_map/reduce_scatter | solution.py:172
  545.1 255.1 %reduce-scatter.12.cloned.1.call-start = ((), (), s32[]{:S(2)}) async-start(), calls=%async_computation.10 | async-start | bytes 2654208 | tf_op jit(solution)/shard_map/reduce_scatter | solution.py:171
  550.4 345.3 %all-reduce.8.cloned.1.call-start = ((), (), s32[]{:S(2)}) async-start(), calls=%async_computation.9 | async-start | bytes 9437184 | tf_op jit(solution)/shard_map/psum | solution.py:167
  554.6 7.4 copy-start.10
  562.1 5.1 copy-start.8
  567.1 18.3 %copy-start.6 = (bf16[3,512,3,64]{1,0,3,2:T(4,128)(2,1)S(1)}, bf16[3,512,3,64]{1,0,3,2:T(4,128)(2,1)}, u32[]{:S(2)}) copy-start(bf16[3,512,3,64]{1,0,3,2:T(4,128)(2,1)} %copy-done.5) | copy-start | bytes 1769476
  604.0 1.2 copy-start.21
  610.9 1.7 copy-start.12
  610.9 355.6 %reduce-scatter.16.cloned.1.call-start = ((), (), s32[]{:S(2)}) async-start(), calls=%async_computation.13 | async-start | bytes 2211840
  619.7 7.9 copy-start.25
  619.7 7.9 copy-start.26
  619.8 37.5 %copy-start.20 = (bf16[192,96]{1,0:T(8,128)(2,1)S(1)}, bf16[192,96]{1,0:T(8,128)(2,1)}, u32[]{:S(2)}) copy-start(bf16[192,96]{1,0:T(8,128)(2,1)} %param.26) | copy-start | bytes 110596
  619.8 108.3 %copy-start.15 = (bf16[768,96]{0,1:T(8,128)(2,1)S(1)}, bf16[768,96]{0,1:T(8,128)(2,1)}, u32[]{:S(2)}) copy-start(bf16[768,96]{0,1:T(8,128)(2,1)} %param.28) | copy-start | bytes 442372
  619.8 180.5 %copy-start.16 = (bf16[96,768]{1,0:T(8,128)(2,1)S(1)}, bf16[96,768]{1,0:T(8,128)(2,1)}, u32[]{:S(2)}) copy-start(bf16[96,768]{1,0:T(8,128)(2,1)} %param.27) | copy-start | bytes 442372
  622.6 177.6 %copy-start.17 = (f32[96,768]{1,0:T(8,128)S(1)}, f32[96,768]{1,0:T(8,128)}, u32[]{:S(2)}) copy-start(f32[96,768]{1,0:T(8,128)} %param.37) | copy-start | bytes 884740
  622.6 177.6 %copy-start.18 = (f32[96,768]{1,0:T(8,128)S(1)}, f32[96,768]{1,0:T(8,128)}, u32[]{:S(2)}) copy-start(f32[96,768]{1,0:T(8,128)} %param.32) | copy-start | bytes 884740
Sparse Core Ops, SparseCore 0:
  100.3 118.9 all-gather.9
  221.6 41.0 all-gather.5
  264.8 39.8 all-gather.7
  311.0 92.7 all-reduce.3
  426.8 94.1 all-reduce.5
  529.8 61.5 reduce-scatter.19
  594.6 61.6 reduce-scatter.17
  660.2 67.8 reduce-scatter.13
  732.0 68.1 reduce-scatter.11
  802.6 93.0 all-reduce.7
  899.6 66.7 reduce-scatter.15
